TPU v7x, 32 devices: a whole 2x2x4 slice. The times are simulated.
32 devices in a mesh: occ: 8 (over y, x, core), vir: 4 (over z).
Axes of the slice: x: 2, y: 2, z: 4, core: 2. Of those that a mesh axis runs over, the one named last changes fastest.
Arguments:
- ints_alpha: bfloat16 [1536, 8, 1024], P('occ', None, 'vir'), may hold values from -0.71875 to 0.71875
- ints_beta: bfloat16 [1536, 8, 1024], P('occ', None, 'vir'), may hold values from -0.71875 to 0.71875
- metric: bfloat16 [1536, 1536], P('vir'), may hold values from -0.5 to 1.5, as said below
- e_occ_alpha: float32 [8], P('occ'), may hold values from -2 to -0.3
- e_occ_beta: float32 [8], replicated, may hold values from -2 to -0.3
- e_vir_alpha: float32 [1024], replicated, may hold values from 0.2 to 3
- e_vir_beta: float32 [1024], P('vir'), may hold values from 0.2 to 3
Outputs:
- gamma_alpha: bfloat16 [1536, 8, 1024], P(None, 'occ', 'vir')
- gamma_beta: bfloat16 [1536, 8, 1024], P(None, 'occ', 'vir')
Inputs may be any that keep to these rules, and one draw needn't show every extreme that they name: `metric`: symmetric and positive definite.
All inputs are finite; a program needn't handle non-finite values.
Results may differ from a plain program's by a relative error of at most 0.009.
Values may be sent and summed in bfloat16 or wider, within the bound.
No kernel may reach another device: no remote copies, remote signals or barrier semaphores. Data moves between devices by JAX's collectives and lax.ppermute only.
A program may use at most 64 MiB of HBM per device.

v0:
```python
import jax
import jax.numpy as jnp
from jax import lax
from jax.sharding import PartitionSpec as P

PAIR_STEPS = 2


def from_partner(value, axis, stride):
    mask = 2**stride
    pairs = [(source, source ^ mask) for source in range(lax.axis_size(axis))]
    return lax.ppermute(value, axis, pairs)


def local(ints_alpha, ints_beta, metric, e_occ_alpha, e_occ_beta, e_vir_alpha, e_vir_beta):
    aux_rows = metric.shape[1]
    occ_dev = e_occ_alpha.shape[0]
    vir_local = e_vir_beta.shape[0]
    vir_total = e_vir_alpha.shape[0]
    alpha_regrouped, beta_regrouped = (
        lax.all_to_all(ints_alpha, "occ", split_axis=1, concat_axis=0, tiled=True),
        lax.all_to_all(ints_beta, "occ", split_axis=1, concat_axis=0, tiled=True),
    )
    stacked = jnp.stack([alpha_regrouped, beta_regrouped], axis=1).reshape(
        aux_rows, 2 * occ_dev * vir_local
    )
    both_rows = jnp.dot(
        lax.all_gather(metric, "vir", axis=0, tiled=True),
        stacked,
        preferred_element_type=jnp.float32,
    ).astype(jnp.bfloat16)
    both_rows = both_rows.reshape(aux_rows, 2, occ_dev, vir_local)
    alpha_whole = lax.all_gather(both_rows[:, 0], "vir", axis=2, tiled=True)
    beta_local = both_rows[:, 1]
    alpha_flat = alpha_whole.reshape(aux_rows, occ_dev * vir_total)
    beta_flat = beta_local.reshape(aux_rows, occ_dev * vir_local)
    left_energy = (e_occ_alpha[:, None] - e_vir_alpha[None, :]).reshape(-1)
    my_block = lax.axis_index("occ")
    hop_bits = list(range(PAIR_STEPS))
    alpha_total = jnp.zeros((aux_rows, occ_dev * vir_total), jnp.float32)
    beta_total = jnp.zeros((aux_rows, occ_dev * vir_local), jnp.float32)
    for hop_bit in hop_bits:
        partner_beta = from_partner(beta_flat, "occ", hop_bit)
        partner = jnp.bitwise_xor(my_block, 1 << hop_bit)
        partner_occ = lax.dynamic_slice_in_dim(e_occ_beta, partner * occ_dev, occ_dev)
        right_energy = (partner_occ[:, None] - e_vir_beta[None, :]).reshape(-1)
        pair_ints = lax.dot_general(
            alpha_flat, partner_beta, (((0,), (0,)), ((), ())), preferred_element_type=jnp.float32
        )
        amplitude = (pair_ints / (left_energy[:, None] + right_energy[None, :])).astype(
            jnp.bfloat16
        )
        alpha_total = alpha_total + lax.dot_general(
            partner_beta, amplitude, (((1,), (1,)), ((), ())), preferred_element_type=jnp.float32
        )
        beta_term = jnp.dot(alpha_flat, amplitude, preferred_element_type=jnp.float32)
        beta_total = beta_total + from_partner(
            beta_term.astype(jnp.bfloat16), "occ", hop_bit
        ).astype(beta_term.dtype)
    gamma_alpha = lax.psum_scatter(
        alpha_total.reshape(aux_rows, occ_dev, vir_total).astype(jnp.bfloat16),
        "vir",
        scatter_dimension=2,
        tiled=True,
    )
    gamma_beta = beta_total.reshape(aux_rows, occ_dev, vir_local)
    return (gamma_alpha, gamma_beta.astype(jnp.bfloat16))


def solution(mesh):
    in_specs = (
        P("occ", None, "vir"),
        P("occ", None, "vir"),
        P("vir", None),
        P("occ"),
        P(),
        P(),
        P("vir"),
    )
    out_specs = (P(None, "occ", "vir"), P(None, "occ", "vir"))
    return jax.shard_map(local, mesh=mesh, in_specs=in_specs, out_specs=out_specs, check_vma=False)
```

profile of v0, /device:TPU:0, one launch (start us, length us, event | category | flops | bytes accessed | tf_op | source)
XLA Modules:
  0.0 244.1 jit_solution(8599499748387885646)
XLA Ops:
  7.2 0.0 copy-start
  7.2 0.0 all-gather.4.cloned.1.call-start
  7.2 0.7 all-gather.4.cloned.1.call-update
  7.9 2.2 copy.9
  10.1 5.2 %all-to-all-start = ((bf16[192,8,256]{2,0,1:T(8,128)(2,1)}), bf16[192,8,256]{2,0,1:T(8,128)(2,1)S(1)}, u32[]{:S(2)}, u32[]{:S(2)}) async-start(bf16[192,8,256]{2,0,1:T(8,128)(2,1)} %copy.9), calls=%async_computation | async-start | bytes 1572864 | tf_op jit(solution)/shard_map/all_to_all | solution.py:21
  15.3 0.0 all-gather.6.cloned.1.call-start
  15.3 0.0 copy-done
  15.3 0.2 copy.10
  15.5 12.3 %all-to-all-done = bf16[192,8,256]{2,0,1:T(8,128)(2,1)S(1)} async-done(((bf16[192,8,256]{2,0,1:T(8,128)(2,1)}), bf16[192,8,256]{2,0,1:T(8,128)(2,1)S(1)}, u32[]{:S(2)}, u32[]{:S(2)}) %all-to-all-start) | async-done | bytes 786464 | tf_op jit(solution)/shard_map/all_to_all | solution.py:21
  27.8 14.9 %all_to_all.30 = bf16[192,8,256]{2,0,1:T(8,128)(2,1)S(1)} all-to-all(bf16[192,8,256]{2,0,1:T(8,128)(2,1)S(1)} %copy.10), channel_id=1, replica_groups=mesh['occ'=8,'vir'=4] {'occ'}, dimensions={1} | all-to-all | bytes 1572864 | tf_op jit(solution)/shard_map/all_to_all | solution.py:22
  42.8 0.1 pad_maximum_fusion
  42.9 0.7 copy.11
  43.6 58.1 %all-gather.4.cloned.1.call-done = bf16[1536,1536]{1,0:T(8,128)(2,1)} async-done(((bf16[384,1536]{1,0:T(8,128)(2,1)}), bf16[1536,1536]{1,0:T(8,128)(2,1)}) %all-gather.4.cloned.1.call-update) | async-done | bytes 4718608 | tf_op jit(solution)/shard_map/all_gather | solution.py:28
  101.7 5.0 %convolution_convert_fusion = bf16[512,1536]{1,0:T(8,128)(2,1)S(1)} fusion(bf16[1536,512]{0,1:T(8,128)(2,1)S(1)} %bitcast.57, bf16[1536,1536]{1,0:T(8,128)(2,1)} %all-gather.4.cloned.1.call-done), kind=kOutput, calls=%fused_computation.10 | convolution fusion | flops 2416705536 | bytes 7864320 | tf_op jit(solution)/shard_map/dot_general | solution.py:27
  106.7 0.0 copy-start.2
  106.7 0.0 copy-start.3
  106.7 0.0 copy-start.1
  106.7 1.0 fusion.28
  107.7 0.0 all-gather.6.cloned.1.call-update
  107.7 0.0 reduce-scatter.2.cloned.1.call-start
  107.8 1.5 collective-permute-start.1
  110.0 0.0 copy-done.2
  110.0 0.6 fusion.29
  110.6 0.0 copy-done.3
  110.6 1.3 broadcast_subtract_fusion.2
  111.8 0.0 copy-done.1
  111.9 0.1 collective-permute-start
  111.9 15.1 %collective-permute-done.1 = bf16[1536,256]{0,1:T(8,128)(2,1)S(1)} collective-permute-done((bf16[1536,256]{0,1:T(8,128)(2,1)S(1)}, bf16[1536,256]{0,1:T(8,128)(2,1)S(1)}, u32[]{:S(2)}, u32[]{:S(2)}) %collective-permute-start.1) | collective-permute-done | bytes 786464 | tf_op jit(solution)/shard_map/ppermute | solution.py:12
  127.0 42.7 %all-gather.6.cloned.1.call-done = bf16[1536,1,1,1024]{0,3,1,2:T(8,128)(2,1)} async-done(((bf16[1536,1,1,256]{0,3,1,2:T(8,128)(2,1)}), bf16[1536,1,1,1024]{0,3,1,2:T(8,128)(2,1)}) %all-gather.6.cloned.1.call-update) | async-done | bytes 3145744 | tf_op jit(solution)/shard_map/all_gather | solution.py:33
  169.7 2.9 %fusion.24 = bf16[1024,256]{1,0:T(8,128)(2,1)S(1)} fusion(bf16[1536,256]{0,1:T(8,128)(2,1)S(1)} %collective-permute-done.1, bf16[1536,1,1,1024]{0,3,1,2:T(8,128)(2,1)} %all-gather.6.cloned.1.call-done, f32[256]{0:T(256)S(1)} %get-tuple-element.5, f32[1024]{0:T(1024)S(1)} %broadcast_subtract_fusion), kind=kOutput, calls=%fused_computation.18 | convolution fusion | flops 806092800 | bytes 4461568 | tf_op jit(solution)/shard_map/dot_general | solution.py:47
  172.6 0.0 copy-start.4
  172.6 1.0 fusion.30
  173.7 0.0 collective-permute-done
  173.7 0.8 copy-done.4
  174.5 1.0 fusion.18
  175.5 2.8 %fusion = bf16[1536,1,1024]{2,0,1:T(8,128)(2,1)} fusion(f32[1536,1024]{1,0:T(8,128)S(1)} %fusion.30, bf16[1536,256]{0,1:T(8,128)(2,1)S(1)} %collective-permute-done, bf16[1024,256]{1,0:T(8,128)(2,1)S(1)} %fusion.18), kind=kOutput, calls=%fused_computation.1 | convolution fusion | flops 808452096 | bytes 10747904 | tf_op jit(solution)/shard_map/dot_general | solution.py:53
  178.3 0.0 reduce-scatter.2.cloned.1.call-update
  178.3 0.0 copy-start.5
  178.3 3.1 %fusion.12 = bf16[1536,256]{1,0:T(8,128)(2,1)S(1)} fusion(bf16[1024,256]{1,0:T(8,128)(2,1)S(1)} %fusion.24, bf16[1536,1,1,1024]{0,3,1,2:T(8,128)(2,1)} %all-gather.6.cloned.1.call-done), kind=kOutput, calls=%fused_computation.12 | convolution fusion | flops 805699584 | bytes 4456448 | tf_op jit(solution)/shard_map/dot_general | solution.py:56
  181.4 1.5 collective-permute-start.3
  183.0 0.0 copy-done.5
  183.0 1.0 fusion.9
  184.0 0.1 collective-permute-start.2
  184.1 16.5 %collective-permute-done.3 = bf16[1536,256]{1,0:T(8,128)(2,1)S(1)} collective-permute-done((bf16[1536,256]{1,0:T(8,128)(2,1)S(1)}, bf16[1536,256]{1,0:T(8,128)(2,1)S(1)}, u32[]{:S(2)}, u32[]{:S(2)}) %collective-permute-start.3) | collective-permute-done | bytes 786464 | tf_op jit(solution)/shard_map/ppermute | solution.py:12
  200.6 0.0 collective-permute-done.2
  200.6 1.1 fusion.27
  201.7 35.8 %reduce-scatter.2.cloned.1.call-done = bf16[1536,1,256]{2,0,1:T(8,128)(2,1)} async-done(((bf16[1536,1,1024]{2,0,1:T(8,128)(2,1)}), bf16[1536,1,256]{2,0,1:T(8,128)(2,1)}) %reduce-scatter.2.cloned.1.call-update) | async-done | bytes 786448 | tf_op jit(solution)/shard_map/reduce_scatter | solution.py:60
  (1 shorter events, 0.0 us)
Async XLA Ops:
  7.2 8.2 %copy-start = (bf16[192,8,256]{2,1,0:T(8,128)(2,1)S(1)}, bf16[192,8,256]{2,1,0:T(8,128)(2,1)}, u32[]{:S(2)}) copy-start(bf16[192,8,256]{2,1,0:T(8,128)(2,1)} %param.8) | copy-start | bytes 2359300
  7.2 94.5 %all-gather.4.cloned.1.call-start = ((), (), s32[]{:S(2)}) async-start(), calls=%async_computation.3 | async-start | bytes 5898240 | tf_op jit(solution)/shard_map/all_gather | solution.py:28
  10.1 17.8 %all-to-all-start = ((bf16[192,8,256]{2,0,1:T(8,128)(2,1)}), bf16[192,8,256]{2,0,1:T(8,128)(2,1)S(1)}, u32[]{:S(2)}, u32[]{:S(2)}) async-start(bf16[192,8,256]{2,0,1:T(8,128)(2,1)} %copy.9), calls=%async_computation | async-start | bytes 1572864 | tf_op jit(solution)/shard_map/all_to_all | solution.py:21
  15.3 154.5 %all-gather.6.cloned.1.call-start = ((), (), s32[]{:S(2)}) async-start(), calls=%async_computation.5 | async-start | bytes 3932160 | tf_op jit(solution)/shard_map/all_gather | solution.py:33
  106.7 3.3 %copy-start.2 = (f32[8]{0:T(128)S(1)}, f32[8]{0:T(128)}, u32[]{:S(2)}) copy-start(f32[8]{0:T(128)} %param.11) | copy-start | bytes 100
  106.7 3.9 %copy-start.3 = (f32[256]{0:T(256)S(1)}, f32[256]{0:T(256)}, u32[]{:S(2)}) copy-start(f32[256]{0:T(256)} %param.13) | copy-start | bytes 3076
  106.7 5.2 %copy-start.1 = (f32[1024]{0:T(1024)S(1)}, f32[1024]{0:T(1024)}, u32[]{:S(2)}) copy-start(f32[1024]{0:T(1024)} %param.12) | copy-start | bytes 12292
  107.7 129.8 %reduce-scatter.2.cloned.1.call-start = ((), (), s32[]{:S(2)}) async-start(), calls=%async_computation.4 | async-start | bytes 3932160 | tf_op jit(solution)/shard_map/reduce_scatter | solution.py:60
  107.8 19.3 %collective-permute-start.1 = (bf16[1536,256]{0,1:T(8,128)(2,1)S(1)}, bf16[1536,256]{0,1:T(8,128)(2,1)S(1)}, u32[]{:S(2)}, u32[]{:S(2)}) collective-permute-start(bf16[1536,256]{0,1:T(8,128)(2,1)S(1)} %get-tuple-element.3), channel_id=1, source_target_pairs={{0,8},{4,12},{8,0},{12,4},{16,24},{20,28},{24,16},{28,20},{1,9},{5... | collective-permute-start | bytes 2359304 | tf_op jit(solution)/shard_map/ppermute | solution.py:12
  111.9 61.8 %collective-permute-start = (bf16[1536,256]{0,1:T(8,128)(2,1)S(1)}, bf16[1536,256]{0,1:T(8,128)(2,1)S(1)}, u32[]{:S(2)}, u32[]{:S(2)}) collective-permute-start(bf16[1536,256]{0,1:T(8,128)(2,1)S(1)} %get-tuple-element.3), channel_id=1, source_target_pairs={{0,4},{4,0},{8,12},{12,8},{16,20},{20,16},{24,28},{28,24},{1,5},{5... | collective-permute-start | bytes 2359304 | tf_op jit(solution)/shard_map/ppermute | solution.py:12
  172.6 1.9 copy-start.4
  178.3 4.6 %copy-start.5 = (bf16[1536,1,1,1024]{0,3,1,2:T(8,128)(2,1)S(1)}, bf16[1536,1,1,1024]{0,3,1,2:T(8,128)(2,1)}, u32[]{:S(2)}) copy-start(bf16[1536,1,1,1024]{0,3,1,2:T(8,128)(2,1)} %all-gather.6.cloned.1.call-done) | copy-start | bytes 9437188
  181.4 19.2 %collective-permute-start.3 = (bf16[1536,256]{1,0:T(8,128)(2,1)S(1)}, bf16[1536,256]{1,0:T(8,128)(2,1)S(1)}, u32[]{:S(2)}, u32[]{:S(2)}) collective-permute-start(bf16[1536,256]{1,0:T(8,128)(2,1)S(1)} %fusion.12), channel_id=1, source_target_pairs={{0,8},{4,12},{8,0},{12,4},{16,24},{20,28},{24,16},{28,20},{1,9},{5... | collective-permute-start | bytes 2359304 | tf_op jit(solution)/shard_map/ppermute | solution.py:12
  184.0 16.6 %collective-permute-start.2 = (bf16[1536,256]{1,0:T(8,128)(2,1)S(1)}, bf16[1536,256]{1,0:T(8,128)(2,1)S(1)}, u32[]{:S(2)}, u32[]{:S(2)}) collective-permute-start(bf16[1536,256]{1,0:T(8,128)(2,1)S(1)} %fusion.9), channel_id=1, source_target_pairs={{0,4},{4,0},{8,12},{12,8},{16,20},{20,16},{24,28},{28,24},{1,5},{5... | collective-permute-start | bytes 2359304 | tf_op jit(solution)/shard_map/ppermute | solution.py:12
Sparse Core Ops, SparseCore 0:
  9.5 92.0 all-gather.3
  107.8 61.8 all-gather.5
  178.5 59.0 reduce-scatter.1
where the time goes:
time: 244 us
  waiting for transfers between devices  181 us (74%)
  matrix products  16.8 us (7%)
  blocking collectives  14.9 us (6%)
  between operations  14.6 us (6%)
  starting transfers between devices  8.53 us (3%)
  local copies, waits for them, and re-layouts  5.48 us (2%)
  other arithmetic  2.52 us (1%)
    all_gather x1, waiting for transfers between devices, local(): lax.all_gather(metric, 'vir', axis=0, tiled=True)  58.1 us
    all_gather x1, waiting for transfers between devices, local(): alpha_whole = lax.all_gather(both_rows[:, 0], 'vir', axis=2, tiled=True)  42.7 us
    reduce_scatter x1, waiting for transfers between devices, local(): lax.psum_scatter(alpha_total.reshape(aux_rows, occ_dev, vir_total).astype...  35.8 us
    ppermute x4, waiting for transfers between devices, from_partner(): return lax.ppermute(value, axis, pairs)  31.6 us
    all_to_all x1, blocking collectives, local(): lax.all_to_all(ints_beta, 'occ', split_axis=1, concat_axis=0, tiled=True)  14.9 us
    all_to_all x1, waiting for transfers between devices, local(): lax.all_to_all(ints_alpha, 'occ', split_axis=1, concat_axis=0, tiled=True)  12.3 us
    all_to_all x1, starting transfers between devices, local(): lax.all_to_all(ints_alpha, 'occ', split_axis=1, concat_axis=0, tiled=True)  5.2 us
    dot_general x1, matrix products, local(): jnp.dot(lax.all_gather(metric, 'vir', axis=0, tiled=True), stacked, prefe...  4.96 us
  transfers between devices with their start and end apart: 8, of which 6 were waited for; matrix products, arithmetic and copies ran while one was open for 6% of the time, Pallas kernels for 0%

commit v1 on v0

--- a/solution.py
+++ b/solution.py
@@ -4,6 +4,27 @@
 from jax.sharding import PartitionSpec as P
 
 PAIR_STEPS = 2
+
+
+def gather_around(x, axis, dim):
+    length, here, rows = (lax.axis_size(axis), lax.axis_index(axis), x.shape[dim])
+    right = [(i, (i + 1) % length) for i in range(length)]
+    left = [(i, (i - 1) % length) for i in range(length)]
+    filled = jnp.zeros((*x.shape[:dim], length * rows, *x.shape[dim + 1 :]), x.dtype)
+    filled = lax.dynamic_update_slice_in_dim(filled, x, here * rows, axis=dim)
+    from_left = from_right = x
+    half = length // 2
+    for step in range(1, half + 1):
+        from_left = lax.ppermute(from_left, axis, right)
+        filled = lax.dynamic_update_slice_in_dim(
+            filled, from_left, (here - step) % length * rows, axis=dim
+        )
+        if step < length - half:
+            from_right = lax.ppermute(from_right, axis, left)
+            filled = lax.dynamic_update_slice_in_dim(
+                filled, from_right, (here + step) % length * rows, axis=dim
+            )
+    return filled
 
 
 def from_partner(value, axis, stride):
@@ -25,9 +46,7 @@
         aux_rows, 2 * occ_dev * vir_local
     )
     both_rows = jnp.dot(
-        lax.all_gather(metric, "vir", axis=0, tiled=True),
-        stacked,
-        preferred_element_type=jnp.float32,
+        gather_around(metric, "vir", 0), stacked, preferred_element_type=jnp.float32
     ).astype(jnp.bfloat16)
     both_rows = both_rows.reshape(aux_rows, 2, occ_dev, vir_local)
     alpha_whole = lax.all_gather(both_rows[:, 0], "vir", axis=2, tiled=True)

time: 244 us -> 236 us (0.967)
  blocking collectives: 14.9 us -> 0 us
  waiting for transfers between devices: 181 us -> 167 us
  local copies, waits for them, and re-layouts: 5.48 us -> 18.3 us
  starting transfers between devices: 8.53 us -> 16 us
    all_gather x1 -> x0, waiting for transfers between devices: 58.1 us -> none  [local(): lax.all_gather(metric, 'vir', axis=0, tiled=True)]
    ppermute x0 -> x3, waiting for transfers between devices: none -> 43.5 us  [the longest x2 26.9 us: gather_around(): from_left = lax.ppermute(from_left, axis, right)]
    all_to_all x1 -> x0, blocking collectives: 14.9 us -> none  [local(): lax.all_to_all(ints_beta, 'occ', split_axis=1, concat_axis=0, tiled=True)]
    dynamic_update_slice x0 -> x4, local copies, waits for them, and re-layouts: none -> 9.51 us  [the longest x2 4.77 us: gather_around(): lax.dynamic_update_slice_in_dim(filled, from_left, (here - step) % length...]
    ppermute x0 -> x3, starting transfers between devices: none -> 5.41 us  [the longest x2 3.11 us: gather_around(): from_left = lax.ppermute(from_left, axis, right)]
    all_gather x1, waiting for transfers between devices: 42.7 us -> 46.5 us  [local(): alpha_whole = lax.all_gather(both_rows[:, 0], 'vir', axis=2, tiled=True)]
    all_to_all x0 -> x1, starting transfers between devices: none -> 3.55 us  [local(): lax.all_to_all(ints_beta, 'occ', split_axis=1, concat_axis=0, tiled=True)]
    broadcast_in_dim x0 -> x1, local copies, waits for them, and re-layouts: none -> 2.45 us  [gather_around(): jnp.zeros((*x.shape[:dim], length * rows, *x.shape[dim + 1:]), x.dtype)]
  transfers between devices with their start and end apart: 8 -> 11, of which waited for: 6 -> 9; matrix products, arithmetic and copies ran while one was open for 6% -> 10% of each run, Pallas kernels for 0% -> 0%
where the time goes in v1:
time: 236 us; the launch traced here: 235 us
  waiting for transfers between devices  167 us (71%)
  local copies, waits for them, and re-layouts  18.3 us (8%)
  matrix products  16.8 us (7%)
  starting transfers between devices  16 us (7%)
  between operations  14.9 us (6%)
  other arithmetic  2.46 us (1%)
    all_gather x1, waiting for transfers between devices, local(): alpha_whole = lax.all_gather(both_rows[:, 0], 'vir', axis=2, tiled=True)  46.5 us
    reduce_scatter x1, waiting for transfers between devices, local(): lax.psum_scatter(alpha_total.reshape(aux_rows, occ_dev, vir_total).astype...  33.9 us
    ppermute x4, waiting for transfers between devices, from_partner(): return lax.ppermute(value, axis, pairs)  30.8 us
    ppermute x2, waiting for transfers between devices, gather_around(): from_left = lax.ppermute(from_left, axis, right)  26.9 us
    ppermute x1, waiting for transfers between devices, gather_around(): from_right = lax.ppermute(from_right, axis, left)  16.7 us
    all_to_all x1, waiting for transfers between devices, local(): lax.all_to_all(ints_alpha, 'occ', split_axis=1, concat_axis=0, tiled=True)  11.5 us
    dot_general x1, matrix products, local(): jnp.dot(gather_around(metric, 'vir', 0), stacked, preferred_element_type=...  4.96 us
    dynamic_update_slice x2, local copies, waits for them, and re-layouts, gather_around(): lax.dynamic_update_slice_in_dim(filled, from_left, (here - step) % length...  4.77 us
  transfers between devices with their start and end apart: 11, of which 9 were waited for; matrix products, arithmetic and copies ran while one was open for 10% of the time, Pallas kernels for 0%

profile of v1, /device:TPU:0, one launch (start us, length us, event | category | flops | bytes accessed | tf_op | source)
XLA Modules:
  0.0 235.2 jit_solution(12493889425961370663)
XLA Ops:
  7.2 3.1 %collective-permute-start = (bf16[384,1536]{1,0:T(8,128)(2,1)}, bf16[384,1536]{1,0:T(8,128)(2,1)}, u32[]{:S(2)}, u32[]{:S(2)}) collective-permute-start(bf16[384,1536]{1,0:T(8,128)(2,1)} %param.9), channel_id=1, source_target_pairs={{0,1},{1,2},{2,3},{3,0},{4,5},{5,6},{6,7},{7,4},{8,9},{9,10},{10,1... | collective-permute-start | bytes 3538952 | tf_op jit(solution)/shard_map/ppermute | solution.py:18
  10.3 2.2 copy.9
  12.4 3.7 %all-to-all-start = ((bf16[192,8,256]{2,0,1:T(8,128)(2,1)}), bf16[192,8,256]{2,0,1:T(8,128)(2,1)S(1)}, u32[]{:S(2)}, u32[]{:S(2)}) async-start(bf16[192,8,256]{2,0,1:T(8,128)(2,1)} %copy.9), calls=%async_computation | async-start | bytes 1572864 | tf_op jit(solution)/shard_map/all_to_all | solution.py:42
  16.2 1.0 copy.10
  17.2 11.5 %all-to-all-done = bf16[192,8,256]{2,0,1:T(8,128)(2,1)S(1)} async-done(((bf16[192,8,256]{2,0,1:T(8,128)(2,1)}), bf16[192,8,256]{2,0,1:T(8,128)(2,1)S(1)}, u32[]{:S(2)}, u32[]{:S(2)}) %all-to-all-start) | async-done | bytes 786464 | tf_op jit(solution)/shard_map/all_to_all | solution.py:42
  28.7 3.5 %all-to-all-start.1 = ((bf16[192,8,256]{2,0,1:T(8,128)(2,1)}), bf16[192,8,256]{2,0,1:T(8,128)(2,1)S(1)}, u32[]{:S(2)}, u32[]{:S(2)}) async-start(bf16[192,8,256]{2,0,1:T(8,128)(2,1)} %copy.10), calls=%async_computation.1 | async-start | bytes 1572864 | tf_op jit(solution)/shard_map/all_to_all | solution.py:43
  32.3 0.0 all-gather.3.cloned.1.call-start
  32.3 2.3 collective-permute-start.1
  34.6 4.8 %collective-permute-done = bf16[384,1536]{1,0:T(8,128)(2,1)} collective-permute-done((bf16[384,1536]{1,0:T(8,128)(2,1)}, bf16[384,1536]{1,0:T(8,128)(2,1)}, u32[]{:S(2)}, u32[]{:S(2)}) %collective-permute-start) | collective-permute-done | bytes 1179680 | tf_op jit(solution)/shard_map/ppermute | solution.py:18
  39.4 0.0 collective-permute-start.2
  39.4 2.4 %broadcast_in_dim.2 = bf16[1536,1536]{1,0:T(8,128)(2,1)} broadcast(bf16[]{:T(256)} %constant.33.clone.1), dimensions={} | broadcast | bytes 4718594 | tf_op jit(solution)/shard_map/broadcast_in_dim | solution.py:13
  41.9 2.4 %constant_dynamic-update-slice_fusion.3 = bf16[1536,1536]{1,0:T(8,128)(2,1)} fusion(bf16[1536,1536]{1,0:T(8,128)(2,1)} %broadcast_in_dim.2, bf16[384,1536]{1,0:T(8,128)(2,1)} %param.9, s32[]{:T(128)S(6)} %select_n.33), kind=kLoop, calls=%fused_computation.25 | loop fusion | bytes 2359300 | tf_op jit(solution)/shard_map/dynamic_update_slice | solution.py:14
  44.3 0.5 all-to-all-done.1
  44.8 0.1 pad_maximum_fusion
  44.9 0.7 copy.11
  45.7 2.4 %constant_dynamic-update-slice_fusion.2 = bf16[1536,1536]{1,0:T(8,128)(2,1)} fusion(bf16[1536,1536]{1,0:T(8,128)(2,1)} %constant_dynamic-update-slice_fusion.3, bf16[384,1536]{1,0:T(8,128)(2,1)} %collective-permute-done, s32[]{:T(128)S(6)} %select_n.35), kind=kLoop, calls=%fused_computation.24 | loop fusion | bytes 2359300 | tf_op jit(solution)/shard_map/dynamic_update_slice | solution.py:19
  48.0 16.7 %collective-permute-done.1 = bf16[384,1536]{1,0:T(8,128)(2,1)} collective-permute-done((bf16[384,1536]{1,0:T(8,128)(2,1)}, bf16[384,1536]{1,0:T(8,128)(2,1)}, u32[]{:S(2)}, u32[]{:S(2)}) %collective-permute-start.1) | collective-permute-done | bytes 1179680 | tf_op jit(solution)/shard_map/ppermute | solution.py:23
  64.7 2.4 %constant_dynamic-update-slice_fusion.1 = bf16[1536,1536]{1,0:T(8,128)(2,1)} fusion(bf16[1536,1536]{1,0:T(8,128)(2,1)} %constant_dynamic-update-slice_fusion.2, bf16[384,1536]{1,0:T(8,128)(2,1)} %collective-permute-done.1, s32[]{:T(128)S(6)} %select_n.37), kind=kLoop, calls=%fused_computation.23 | loop fusion | bytes 2359300 | tf_op jit(solution)/shard_map/dynamic_update_slice | solution.py:24
  67.1 22.1 %collective-permute-done.2 = bf16[384,1536]{1,0:T(8,128)(2,1)} collective-permute-done((bf16[384,1536]{1,0:T(8,128)(2,1)}, bf16[384,1536]{1,0:T(8,128)(2,1)}, u32[]{:S(2)}, u32[]{:S(2)}) %collective-permute-start.2) | collective-permute-done | bytes 1179680 | tf_op jit(solution)/shard_map/ppermute | solution.py:18
  89.2 2.4 %constant_dynamic-update-slice_fusion = bf16[1536,1536]{1,0:T(8,128)(2,1)} fusion(bf16[1536,1536]{1,0:T(8,128)(2,1)} %constant_dynamic-update-slice_fusion.1, bf16[384,1536]{1,0:T(8,128)(2,1)} %collective-permute-done.2, s32[]{:T(128)S(6)} %select_n.39), kind=kLoop, calls=%fused_computation.22 | loop fusion | bytes 2359300 | tf_op jit(solution)/shard_map/dynamic_update_slice | solution.py:19
  91.5 5.0 %convolution_convert_fusion = bf16[1536,512]{0,1:T(8,128)(2,1)S(1)} fusion(bf16[1536,1536]{1,0:T(8,128)(2,1)} %constant_dynamic-update-slice_fusion, bf16[1536,512]{0,1:T(8,128)(2,1)S(1)} %bitcast.55), kind=kOutput, calls=%fused_computation.10 | convolution fusion | flops 2416705536 | bytes 7864320 | tf_op jit(solution)/shard_map/dot_general | solution.py:48
  96.5 0.0 copy-start.2
  96.5 0.0 copy-start.3
  96.5 0.0 copy-start.1
  96.5 1.0 fusion.28
  97.5 0.0 all-gather.3.cloned.1.call-update
  97.5 0.0 reduce-scatter.2.cloned.1.call-start
  97.6 1.6 collective-permute-start.4
  99.8 0.6 fusion.29
  100.4 1.2 broadcast_subtract_fusion.2
  101.7 0.1 collective-permute-start.3
  101.7 12.3 %collective-permute-done.4 = bf16[1536,256]{0,1:T(8,128)(2,1)S(1)} collective-permute-done((bf16[1536,256]{0,1:T(8,128)(2,1)S(1)}, bf16[1536,256]{0,1:T(8,128)(2,1)S(1)}, u32[]{:S(2)}, u32[]{:S(2)}) %collective-permute-start.4) | collective-permute-done | bytes 786464 | tf_op jit(solution)/shard_map/ppermute | solution.py:33
  114.0 46.5 %all-gather.3.cloned.1.call-done = bf16[1536,1,1,1024]{0,3,1,2:T(8,128)(2,1)} async-done(((bf16[1536,1,1,256]{0,3,1,2:T(8,128)(2,1)}), bf16[1536,1,1,1024]{0,3,1,2:T(8,128)(2,1)}) %all-gather.3.cloned.1.call-update) | async-done | bytes 3145744 | tf_op jit(solution)/shard_map/all_gather | solution.py:52
  160.5 2.9 %fusion.24 = bf16[1024,256]{1,0:T(8,128)(2,1)S(1)} fusion(bf16[1536,256]{0,1:T(8,128)(2,1)S(1)} %collective-permute-done.4, bf16[1536,1,1,1024]{0,3,1,2:T(8,128)(2,1)} %all-gather.3.cloned.1.call-done, f32[256]{0:T(256)S(1)} %get-tuple-element.5, f32[1024]{0:T(1024)S(1)} %broadcast_subtract_fusion), kind=kOutput, calls=%fused_computation.18 | convolution fusion | flops 806092800 | bytes 4461568 | tf_op jit(solution)/shard_map/dot_general | solution.py:66
  163.4 1.0 fusion.30
  164.5 0.0 collective-permute-done.3
  164.5 0.8 copy-done.4
  165.3 1.0 fusion.18
  166.3 2.8 %fusion = bf16[1536,1,1024]{2,0,1:T(8,128)(2,1)} fusion(f32[1536,1024]{1,0:T(8,128)S(1)} %fusion.30, bf16[1536,256]{0,1:T(8,128)(2,1)S(1)} %collective-permute-done.3, bf16[1024,256]{1,0:T(8,128)(2,1)S(1)} %fusion.18), kind=kOutput, calls=%fused_computation.1 | convolution fusion | flops 808452096 | bytes 10747904 | tf_op jit(solution)/shard_map/dot_general | solution.py:72
  169.1 0.0 reduce-scatter.2.cloned.1.call-update
  169.1 3.1 %fusion.9 = bf16[1536,256]{1,0:T(8,128)(2,1)S(1)} fusion(bf16[1024,256]{1,0:T(8,128)(2,1)S(1)} %fusion.18, bf16[1536,1,1,1024]{0,3,1,2:T(8,128)(2,1)} %all-gather.3.cloned.1.call-done), kind=kOutput, calls=%fused_computation.11 | convolution fusion | flops 805699584 | bytes 4456448 | tf_op jit(solution)/shard_map/dot_general | solution.py:75
  172.2 0.1 collective-permute-start.5
  172.3 1.0 fusion.12
  173.3 1.5 collective-permute-start.6
  174.9 0.0 collective-permute-done.5
  174.9 18.5 %collective-permute-done.6 = bf16[1536,256]{1,0:T(8,128)(2,1)S(1)} collective-permute-done((bf16[1536,256]{1,0:T(8,128)(2,1)S(1)}, bf16[1536,256]{1,0:T(8,128)(2,1)S(1)}, u32[]{:S(2)}, u32[]{:S(2)}) %collective-permute-start.6) | collective-permute-done | bytes 786464 | tf_op jit(solution)/shard_map/ppermute | solution.py:33
  193.3 1.1 fusion.27
  194.4 33.9 %reduce-scatter.2.cloned.1.call-done = bf16[1536,1,256]{2,0,1:T(8,128)(2,1)} async-done(((bf16[1536,1,1024]{2,0,1:T(8,128)(2,1)}), bf16[1536,1,256]{2,0,1:T(8,128)(2,1)}) %reduce-scatter.2.cloned.1.call-update) | async-done | bytes 786448 | tf_op jit(solution)/shard_map/reduce_scatter | solution.py:79
  (9 shorter events, 0.0 us)
Async XLA Ops:
  7.2 9.0 %copy-start = (bf16[192,8,256]{2,1,0:T(8,128)(2,1)S(1)}, bf16[192,8,256]{2,1,0:T(8,128)(2,1)}, u32[]{:S(2)}) copy-start(bf16[192,8,256]{2,1,0:T(8,128)(2,1)} %param.8) | copy-start | bytes 2359300
  7.2 32.3 %collective-permute-start = (bf16[384,1536]{1,0:T(8,128)(2,1)}, bf16[384,1536]{1,0:T(8,128)(2,1)}, u32[]{:S(2)}, u32[]{:S(2)}) collective-permute-start(bf16[384,1536]{1,0:T(8,128)(2,1)} %param.9), channel_id=1, source_target_pairs={{0,1},{1,2},{2,3},{3,0},{4,5},{5,6},{6,7},{7,4},{8,9},{9,10},{10,1... | collective-permute-start | bytes 3538952 | tf_op jit(solution)/shard_map/ppermute | solution.py:18
  12.4 16.3 %all-to-all-start = ((bf16[192,8,256]{2,0,1:T(8,128)(2,1)}), bf16[192,8,256]{2,0,1:T(8,128)(2,1)S(1)}, u32[]{:S(2)}, u32[]{:S(2)}) async-start(bf16[192,8,256]{2,0,1:T(8,128)(2,1)} %copy.9), calls=%async_computation | async-start | bytes 1572864 | tf_op jit(solution)/shard_map/all_to_all | solution.py:42
  28.7 16.1 %all-to-all-start.1 = ((bf16[192,8,256]{2,0,1:T(8,128)(2,1)}), bf16[192,8,256]{2,0,1:T(8,128)(2,1)S(1)}, u32[]{:S(2)}, u32[]{:S(2)}) async-start(bf16[192,8,256]{2,0,1:T(8,128)(2,1)} %copy.10), calls=%async_computation.1 | async-start | bytes 1572864 | tf_op jit(solution)/shard_map/all_to_all | solution.py:43
  32.3 128.2 %all-gather.3.cloned.1.call-start = ((), (), s32[]{:S(2)}) async-start(), calls=%async_computation.4 | async-start | bytes 3932160 | tf_op jit(solution)/shard_map/all_gather | solution.py:52
  32.3 32.4 %collective-permute-start.1 = (bf16[384,1536]{1,0:T(8,128)(2,1)}, bf16[384,1536]{1,0:T(8,128)(2,1)}, u32[]{:S(2)}, u32[]{:S(2)}) collective-permute-start(bf16[384,1536]{1,0:T(8,128)(2,1)} %param.9), channel_id=1, source_target_pairs={{0,3},{1,0},{2,1},{3,2},{4,7},{5,4},{6,5},{7,6},{8,11},{9,8},{10,9... | collective-permute-start | bytes 3538952 | tf_op jit(solution)/shard_map/ppermute | solution.py:23
  39.4 49.7 %collective-permute-start.2 = (bf16[384,1536]{1,0:T(8,128)(2,1)}, bf16[384,1536]{1,0:T(8,128)(2,1)}, u32[]{:S(2)}, u32[]{:S(2)}) collective-permute-start(bf16[384,1536]{1,0:T(8,128)(2,1)} %collective-permute-done), channel_id=1, source_target_pairs={{0,1},{1,2},{2,3},{3,0},{4,5},{5,6},{6,7},{7,4},{8,9},{9,10},{10,1... | collective-permute-start | bytes 3538952 | tf_op jit(solution)/shard_map/ppermute | solution.py:18
  96.5 3.3 %copy-start.2 = (f32[8]{0:T(128)S(1)}, f32[8]{0:T(128)}, u32[]{:S(2)}) copy-start(f32[8]{0:T(128)} %param.11) | copy-start | bytes 100
  96.5 3.9 %copy-start.3 = (f32[256]{0:T(256)S(1)}, f32[256]{0:T(256)}, u32[]{:S(2)}) copy-start(f32[256]{0:T(256)} %param.13) | copy-start | bytes 3076
  96.5 5.1 %copy-start.1 = (f32[1024]{0:T(1024)S(1)}, f32[1024]{0:T(1024)}, u32[]{:S(2)}) copy-start(f32[1024]{0:T(1024)} %param.12) | copy-start | bytes 12292
  97.5 130.8 %reduce-scatter.2.cloned.1.call-start = ((), (), s32[]{:S(2)}) async-start(), calls=%async_computation.3 | async-start | bytes 3932160 | tf_op jit(solution)/shard_map/reduce_scatter | solution.py:79
  97.6 16.5 %collective-permute-start.4 = (bf16[1536,256]{0,1:T(8,128)(2,1)S(1)}, bf16[1536,256]{0,1:T(8,128)(2,1)S(1)}, u32[]{:S(2)}, u32[]{:S(2)}) collective-permute-start(bf16[1536,256]{0,1:T(8,128)(2,1)S(1)} %get-tuple-element.3), channel_id=1, source_target_pairs={{0,8},{4,12},{8,0},{12,4},{16,24},{20,28},{24,16},{28,20},{1,9},{5... | collective-permute-start | bytes 2359304 | tf_op jit(solution)/shard_map/ppermute | solution.py:33
  101.7 62.8 %collective-permute-start.3 = (bf16[1536,256]{0,1:T(8,128)(2,1)S(1)}, bf16[1536,256]{0,1:T(8,128)(2,1)S(1)}, u32[]{:S(2)}, u32[]{:S(2)}) collective-permute-start(bf16[1536,256]{0,1:T(8,128)(2,1)S(1)} %get-tuple-element.3), channel_id=1, source_target_pairs={{0,4},{4,0},{8,12},{12,8},{16,20},{20,16},{24,28},{28,24},{1,5},{5... | collective-permute-start | bytes 2359304 | tf_op jit(solution)/shard_map/ppermute | solution.py:33
  163.4 1.9 copy-start.4
  169.1 3.2 %copy-start.5 = (bf16[1536,1,1,1024]{0,3,1,2:T(8,128)(2,1)S(1)}, bf16[1536,1,1,1024]{0,3,1,2:T(8,128)(2,1)}, u32[]{:S(2)}) copy-start(bf16[1536,1,1,1024]{0,3,1,2:T(8,128)(2,1)} %all-gather.3.cloned.1.call-done) | copy-start | bytes 9437188
  172.2 2.7 %collective-permute-start.5 = (bf16[1536,256]{1,0:T(8,128)(2,1)S(1)}, bf16[1536,256]{1,0:T(8,128)(2,1)S(1)}, u32[]{:S(2)}, u32[]{:S(2)}) collective-permute-start(bf16[1536,256]{1,0:T(8,128)(2,1)S(1)} %fusion.9), channel_id=1, source_target_pairs={{0,4},{4,0},{8,12},{12,8},{16,20},{20,16},{24,28},{28,24},{1,5},{5... | collective-permute-start | bytes 2359304 | tf_op jit(solution)/shard_map/ppermute | solution.py:33
  173.3 20.0 %collective-permute-start.6 = (bf16[1536,256]{1,0:T(8,128)(2,1)S(1)}, bf16[1536,256]{1,0:T(8,128)(2,1)S(1)}, u32[]{:S(2)}, u32[]{:S(2)}) collective-permute-start(bf16[1536,256]{1,0:T(8,128)(2,1)S(1)} %fusion.12), channel_id=1, source_target_pairs={{0,8},{4,12},{8,0},{12,4},{16,24},{20,28},{24,16},{28,20},{1,9},{5... | collective-permute-start | bytes 2359304 | tf_op jit(solution)/shard_map/ppermute | solution.py:33
Sparse Core Ops, SparseCore 0:
  97.7 62.7 all-gather.2
  169.2 59.0 reduce-scatter.1
